TPU v7x, 32 devices: a whole 2x2x4 slice. The times are simulated.
32 devices in a mesh: grp: 2 (over x), row: 16 (over z, y, core).
Axes of the slice: x: 2, y: 2, z: 4, core: 2. Of those that a mesh axis runs over, the one named last changes fastest.
Arguments:
- coordinates: float32 [3, 65536], P(None, ('grp', 'row')), parts along dimension 1, may hold values from -0.12 to 1.12, as said below
- length_scale: float32 [65536], P(('grp', 'row')), parts along dimension 0, may hold values from 0.05 to 0.4
- probes: bfloat16 [64, 65536], P(None, ('grp', 'row')), parts along dimension 1, may hold values from -6 to 6
- near_ids: int32 [256, 16], P(('grp', 'row')), parts along dimension 0, may hold values from 0 to 127, as said below
- near_count: int32 [256], P(('grp', 'row')), parts along dimension 0, may hold values from 8 to 16
- basis_out: bfloat16 [256, 32, 256], P(('grp', 'row')), parts along dimension 0, may hold values from -1 to 1
- basis_in: bfloat16 [256, 32, 256], P(('grp', 'row')), parts along dimension 0, may hold values from -0.375 to 0.375
Outputs:
- sampled: float32 [64, 65536], P(None, ('grp', 'row')), parts along dimension 1
There are 2 independent parts, one for each index of `grp`. A program takes and returns all parts, laid end to end along the dimension named above; each array names one. Nothing has to cross between parts.
Inputs may be any that keep to these rules, and one draw needn't show every extreme that they name: `coordinates`: points of one block lie within 0.12 of a common center in every coordinate. `near_ids`: row i lists i itself first, then distinct blocks whose index differs from i by at most 8; the slots from near_count[i] on hold i again.
All inputs are finite; a program needn't handle non-finite values.
Results may differ from a plain program's by a relative error of at most 0.00055.
The roundings to bfloat16 on the way count: a program that leaves them out, or rounds other values in their place, can miss the bound.
Values may be sent and summed in bfloat16 or wider, within the bound.
A program may use at most 64 MiB of HBM per device.

v0:
```python
import jax
import jax.numpy as jnp
from jax import lax
from jax.sharding import PartitionSpec as P

HALO = 8


def with_halo(cells, sides, width):
    for axis, dim in sides:
        count = lax.axis_size(axis)
        ends = count - 1
        head = lax.slice_in_dim(cells, 0, width, axis=dim)
        tail = lax.slice_in_dim(cells, cells.shape[dim] - width, cells.shape[dim], axis=dim)
        cells = jnp.concatenate(
            [
                lax.ppermute(tail, axis, [(i, (i + 1) % count) for i in range(ends)]),
                cells,
                lax.ppermute(head, axis, [((i + 1) % count, i) for i in range(ends)]),
            ],
            axis=dim,
        )
    return cells


def matern(first, second):
    sq_dist = (first[0] - second[0]) * (first[0] - second[0])
    sq_dist = sq_dist + (first[1] - second[1]) * (first[1] - second[1])
    sq_dist = sq_dist + (first[2] - second[2]) * (first[2] - second[2])
    mean_sq = 0.5 * (first[3] * first[3] + second[3] * second[3])
    prefac = (first[3] * second[3] / mean_sq) ** 1.5
    scaled = jnp.sqrt(3.0) * jnp.sqrt(sq_dist / mean_sq)
    return prefac * (1.0 + scaled) * jnp.exp(-scaled)


def shards(coordinates, length_scale, probes, near_ids, near_count, basis_out, basis_in):
    block_size = basis_out.shape[2]
    own_blocks = basis_out.shape[0]
    rank_size = basis_out.shape[1]
    probe_size = probes.shape[0]
    first_block = lax.axis_index("row") * own_blocks
    records = jnp.concatenate([coordinates, length_scale[None, :]], axis=0)
    wide_records = with_halo(records, (("row", 1),), HALO * block_size)
    wide_probes = with_halo(probes, (("row", 1),), HALO * block_size)
    wide_count = own_blocks + 2 * HALO
    rec_blocks = wide_records.reshape(4, wide_count, block_size)
    probe_blocks = wide_probes.reshape(probe_size, wide_count, block_size)
    own_records = records.reshape(4, own_blocks, block_size)
    own_probes = probes.reshape(probe_size, own_blocks, block_size)

    def near_step(total, inputs):
        column_ids, column_index = inputs
        local_ids = column_ids - first_block + HALO
        source = jnp.take(rec_blocks, local_ids, axis=1)
        tiles = matern(source[:, :, :, None], own_records[:, :, None, :])
        keep = (column_index < near_count).astype(jnp.float32)
        tiles = (tiles * keep[:, None, None]).astype(jnp.bfloat16)
        source_probe = jnp.take(probe_blocks, local_ids, axis=1)
        update = jnp.einsum("pra,rab->prb", source_probe, tiles, preferred_element_type=jnp.float32)
        return (total + update, None)

    start_near = jnp.zeros((probe_size, own_blocks, block_size), jnp.float32)
    columns = jnp.arange(near_ids.shape[1])
    near, _ = lax.scan(near_step, start_near, (near_ids.T, columns))
    folded = jnp.einsum("rkb,prb->rkp", basis_in, own_probes, preferred_element_type=jnp.float32)
    folded = folded.astype(jnp.bfloat16).reshape(own_blocks, rank_size * probe_size)
    own_center = jnp.mean(own_records, axis=2)
    all_centers = lax.all_gather(own_center, "row", axis=1, tiled=True)
    piece = lax.all_gather(folded, "row", axis=0, tiled=True)
    width = piece.shape[0]
    coupling = matern(own_center[:, :, None], all_centers[:, None, :])
    global_ids = jnp.arange(width)
    is_near = jnp.any(near_ids[:, :, None] == global_ids[None, None, :], axis=1)
    coupling = jnp.where(is_near, 0.0, coupling).astype(jnp.bfloat16)
    summed = jnp.dot(coupling, piece, preferred_element_type=jnp.float32)
    summed = summed.astype(jnp.bfloat16).reshape(own_blocks, rank_size, probe_size)
    far = jnp.einsum("rkp,rkb->prb", summed, basis_out, preferred_element_type=jnp.float32)
    return (near + far).reshape(probe_size, own_blocks * block_size)


def solution(mesh):
    placed = (
        P(None, ("grp", "row")),
        P(("grp", "row")),
        P(None, ("grp", "row")),
        P(("grp", "row"), None),
        P(("grp", "row")),
        P(("grp", "row"), None, None),
        P(("grp", "row"), None, None),
    )
    return jax.shard_map(
        shards, mesh=mesh, in_specs=placed, out_specs=P(None, ("grp", "row")), check_vma=False
    )
```

profile of v0, /device:TPU:0, one launch (start us, length us, event | category | flops | bytes accessed | tf_op | source)
XLA Modules:
  0.0 174.5 jit_solution(7087725356720099035)
XLA Ops:
  0.0 0.8 pad_maximum_fusion.2
  0.8 1.3 collective-permute-start.1
  2.1 3.0 %collective-permute-start = (f32[4,2048]{1,0:T(4,128)S(1)}, f32[4,2048]{1,0:T(4,128)S(1)}, u32[]{:S(2)}, u32[]{:S(2)}) collective-permute-start(f32[4,2048]{1,0:T(4,128)S(1)} %pad_maximum_fusion.2), channel_id=1, source_target_pairs={{0,1},{1,2},{2,3},{3,4},{4,5},{5,6},{6,7},{7,8},{8,9},{9,10},{10,1... | collective-permute-start | bytes 98312 | tf_op jit(solution)/shard_map/ppermute | solution.py:17
  5.2 1.3 collective-permute-start.3
  6.5 5.2 %collective-permute-start.2 = (bf16[64,2048]{1,0:T(8,128)(2,1)}, bf16[64,2048]{1,0:T(8,128)(2,1)S(1)}, u32[]{:S(2)}, u32[]{:S(2)}) collective-permute-start(bf16[64,2048]{1,0:T(8,128)(2,1)} %param.11), channel_id=1, source_target_pairs={{0,1},{1,2},{2,3},{3,4},{4,5},{5,6},{6,7},{7,8},{8,9},{9,10},{10,1... | collective-permute-start | bytes 786440 | tf_op jit(solution)/shard_map/ppermute | solution.py:17
  11.7 0.7 concatenate.20
  12.4 0.8 copy.55
  13.2 1.2 convolution_convert_fusion.1
  14.6 23.3 %all_gather.7 = bf16[128,2048]{1,0:T(8,128)(2,1)S(1)} all-gather(bf16[8,2048]{1,0:T(8,128)(2,1)S(1)} %reshape.154), channel_id=1, replica_groups=mesh['grp'=2,'row'=16] {'row'}, dimensions={0}, use_global_device_ids=true | all-gather | bytes 557056 | tf_op jit(solution)/shard_map/all_gather | solution.py:69
  38.0 17.5 %all-gather = f32[16,8,4]{1,2,0:T(4,128)S(1)} all-gather(f32[1,8,4]{1,2,0:T(4,128)S(1)} %get-tuple-element.228), channel_id=1, replica_groups=mesh['grp'=2,'row'=16] {'row'}, dimensions={0}, use_global_device_ids=true | all-gather | bytes 2176 | tf_op jit(solution)/shard_map/all_gather | solution.py:68
  57.0 116.4 %while.13 = (s32[]{:T(128)}, f32[64,8,256]{2,0,1:T(8,128)S(1)}, s32[16,8]{1,0:T(8,128)S(1)}, s32[]{:T(128)}, f32[4,24,256]{2,0,1:T(4,128)S(1)}, /*index=5*/f32[4...) while((s32[]{:T(128)}, f32[64,8,256]{2,0,1:T(8,128)S(1)}, ...), condition=%wide.region_1.2_spmd.clone, body=%wide.region_0.1_spmd.clone.sunk | while | flops 77999224 | bytes 2331103 | solution.py:64
  57.0 0.6 dynamic_slice.24
  57.6 0.6 compare_convert_fusion.2
  58.3 0.6 gather_fusion
  59.6 4.6 %fusion.68 = f32[64,8,256]{2,0,1:T(8,128)S(1)} fusion(f32[8]{0:T(128)S(1)} %get-tuple-element.300, f32[8,256]{1,0:T(8,128)S(1)} %sub.339, f32[8,256]{1,0:T(8,128)S(1)} %bitcast.123, f32[8,256]{1,0:T(8,128)S(1)} %sub.340, f32[8,256]{1,0:T(8,128)S(1)} %bitcast.124, f32[8,256]{1,0:T(8,128)S(1)} %sub.341, f32[8,256]{1,0:T(8,128)S(1)} %bitcast.125, ...), kind=kOutput, calls=%fused_computation.4.clone.1 | convolution fusion | flops 77987840 | bytes 1392681 | tf_op jit(solution)/shard_map/while/body/eval_jaxpr/pra,rab->prb/dot_general | solution.py:59
  64.2 0.6 dynamic_slice.24
  64.8 0.6 compare_convert_fusion.2
  65.6 0.6 gather_fusion
  66.9 4.6 %fusion.68 = f32[64,8,256]{2,0,1:T(8,128)S(1)} fusion(f32[8]{0:T(128)S(1)} %get-tuple-element.300, f32[8,256]{1,0:T(8,128)S(1)} %sub.339, f32[8,256]{1,0:T(8,128)S(1)} %bitcast.123, f32[8,256]{1,0:T(8,128)S(1)} %sub.340, f32[8,256]{1,0:T(8,128)S(1)} %bitcast.124, f32[8,256]{1,0:T(8,128)S(1)} %sub.341, f32[8,256]{1,0:T(8,128)S(1)} %bitcast.125, ...), kind=kOutput, calls=%fused_computation.4.clone.1 | convolution fusion | flops 77987840 | bytes 1392681 | tf_op jit(solution)/shard_map/while/body/eval_jaxpr/pra,rab->prb/dot_general | solution.py:59
  71.5 0.6 dynamic_slice.24
  72.1 0.6 compare_convert_fusion.2
  72.8 0.6 gather_fusion
  74.2 4.6 %fusion.68 = f32[64,8,256]{2,0,1:T(8,128)S(1)} fusion(f32[8]{0:T(128)S(1)} %get-tuple-element.300, f32[8,256]{1,0:T(8,128)S(1)} %sub.339, f32[8,256]{1,0:T(8,128)S(1)} %bitcast.123, f32[8,256]{1,0:T(8,128)S(1)} %sub.340, f32[8,256]{1,0:T(8,128)S(1)} %bitcast.124, f32[8,256]{1,0:T(8,128)S(1)} %sub.341, f32[8,256]{1,0:T(8,128)S(1)} %bitcast.125, ...), kind=kOutput, calls=%fused_computation.4.clone.1 | convolution fusion | flops 77987840 | bytes 1392681 | tf_op jit(solution)/shard_map/while/body/eval_jaxpr/pra,rab->prb/dot_general | solution.py:59
  78.8 0.6 dynamic_slice.24
  79.4 0.6 compare_convert_fusion.2
  80.1 0.6 gather_fusion
  81.5 4.6 %fusion.68 = f32[64,8,256]{2,0,1:T(8,128)S(1)} fusion(f32[8]{0:T(128)S(1)} %get-tuple-element.300, f32[8,256]{1,0:T(8,128)S(1)} %sub.339, f32[8,256]{1,0:T(8,128)S(1)} %bitcast.123, f32[8,256]{1,0:T(8,128)S(1)} %sub.340, f32[8,256]{1,0:T(8,128)S(1)} %bitcast.124, f32[8,256]{1,0:T(8,128)S(1)} %sub.341, f32[8,256]{1,0:T(8,128)S(1)} %bitcast.125, ...), kind=kOutput, calls=%fused_computation.4.clone.1 | convolution fusion | flops 77987840 | bytes 1392681 | tf_op jit(solution)/shard_map/while/body/eval_jaxpr/pra,rab->prb/dot_general | solution.py:59
  86.1 0.6 dynamic_slice.24
  87.4 0.6 gather_fusion
  88.7 4.6 %fusion.68 = f32[64,8,256]{2,0,1:T(8,128)S(1)} fusion(f32[8]{0:T(128)S(1)} %get-tuple-element.300, f32[8,256]{1,0:T(8,128)S(1)} %sub.339, f32[8,256]{1,0:T(8,128)S(1)} %bitcast.123, f32[8,256]{1,0:T(8,128)S(1)} %sub.340, f32[8,256]{1,0:T(8,128)S(1)} %bitcast.124, f32[8,256]{1,0:T(8,128)S(1)} %sub.341, f32[8,256]{1,0:T(8,128)S(1)} %bitcast.125, ...), kind=kOutput, calls=%fused_computation.4.clone.1 | convolution fusion | flops 77987840 | bytes 1392681 | tf_op jit(solution)/shard_map/while/body/eval_jaxpr/pra,rab->prb/dot_general | solution.py:59
  93.4 0.6 dynamic_slice.24
  94.7 0.6 gather_fusion
  96.0 4.6 %fusion.68 = f32[64,8,256]{2,0,1:T(8,128)S(1)} fusion(f32[8]{0:T(128)S(1)} %get-tuple-element.300, f32[8,256]{1,0:T(8,128)S(1)} %sub.339, f32[8,256]{1,0:T(8,128)S(1)} %bitcast.123, f32[8,256]{1,0:T(8,128)S(1)} %sub.340, f32[8,256]{1,0:T(8,128)S(1)} %bitcast.124, f32[8,256]{1,0:T(8,128)S(1)} %sub.341, f32[8,256]{1,0:T(8,128)S(1)} %bitcast.125, ...), kind=kOutput, calls=%fused_computation.4.clone.1 | convolution fusion | flops 77987840 | bytes 1392681 | tf_op jit(solution)/shard_map/while/body/eval_jaxpr/pra,rab->prb/dot_general | solution.py:59
  100.6 0.6 dynamic_slice.24
  101.9 0.6 gather_fusion
  103.3 4.6 %fusion.68 = f32[64,8,256]{2,0,1:T(8,128)S(1)} fusion(f32[8]{0:T(128)S(1)} %get-tuple-element.300, f32[8,256]{1,0:T(8,128)S(1)} %sub.339, f32[8,256]{1,0:T(8,128)S(1)} %bitcast.123, f32[8,256]{1,0:T(8,128)S(1)} %sub.340, f32[8,256]{1,0:T(8,128)S(1)} %bitcast.124, f32[8,256]{1,0:T(8,128)S(1)} %sub.341, f32[8,256]{1,0:T(8,128)S(1)} %bitcast.125, ...), kind=kOutput, calls=%fused_computation.4.clone.1 | convolution fusion | flops 77987840 | bytes 1392681 | tf_op jit(solution)/shard_map/while/body/eval_jaxpr/pra,rab->prb/dot_general | solution.py:59
  107.9 0.6 dynamic_slice.24
  109.2 0.6 gather_fusion
  110.6 4.6 %fusion.68 = f32[64,8,256]{2,0,1:T(8,128)S(1)} fusion(f32[8]{0:T(128)S(1)} %get-tuple-element.300, f32[8,256]{1,0:T(8,128)S(1)} %sub.339, f32[8,256]{1,0:T(8,128)S(1)} %bitcast.123, f32[8,256]{1,0:T(8,128)S(1)} %sub.340, f32[8,256]{1,0:T(8,128)S(1)} %bitcast.124, f32[8,256]{1,0:T(8,128)S(1)} %sub.341, f32[8,256]{1,0:T(8,128)S(1)} %bitcast.125, ...), kind=kOutput, calls=%fused_computation.4.clone.1 | convolution fusion | flops 77987840 | bytes 1392681 | tf_op jit(solution)/shard_map/while/body/eval_jaxpr/pra,rab->prb/dot_general | solution.py:59
  115.2 0.6 dynamic_slice.24
  116.5 0.6 gather_fusion
  117.8 4.6 %fusion.68 = f32[64,8,256]{2,0,1:T(8,128)S(1)} fusion(f32[8]{0:T(128)S(1)} %get-tuple-element.300, f32[8,256]{1,0:T(8,128)S(1)} %sub.339, f32[8,256]{1,0:T(8,128)S(1)} %bitcast.123, f32[8,256]{1,0:T(8,128)S(1)} %sub.340, f32[8,256]{1,0:T(8,128)S(1)} %bitcast.124, f32[8,256]{1,0:T(8,128)S(1)} %sub.341, f32[8,256]{1,0:T(8,128)S(1)} %bitcast.125, ...), kind=kOutput, calls=%fused_computation.4.clone.1 | convolution fusion | flops 77987840 | bytes 1392681 | tf_op jit(solution)/shard_map/while/body/eval_jaxpr/pra,rab->prb/dot_general | solution.py:59
  122.5 0.6 dynamic_slice.24
  123.8 0.6 gather_fusion
  125.1 4.6 %fusion.68 = f32[64,8,256]{2,0,1:T(8,128)S(1)} fusion(f32[8]{0:T(128)S(1)} %get-tuple-element.300, f32[8,256]{1,0:T(8,128)S(1)} %sub.339, f32[8,256]{1,0:T(8,128)S(1)} %bitcast.123, f32[8,256]{1,0:T(8,128)S(1)} %sub.340, f32[8,256]{1,0:T(8,128)S(1)} %bitcast.124, f32[8,256]{1,0:T(8,128)S(1)} %sub.341, f32[8,256]{1,0:T(8,128)S(1)} %bitcast.125, ...), kind=kOutput, calls=%fused_computation.4.clone.1 | convolution fusion | flops 77987840 | bytes 1392681 | tf_op jit(solution)/shard_map/while/body/eval_jaxpr/pra,rab->prb/dot_general | solution.py:59
  129.7 0.6 dynamic_slice.24
  131.0 0.6 gather_fusion
  132.4 4.6 %fusion.68 = f32[64,8,256]{2,0,1:T(8,128)S(1)} fusion(f32[8]{0:T(128)S(1)} %get-tuple-element.300, f32[8,256]{1,0:T(8,128)S(1)} %sub.339, f32[8,256]{1,0:T(8,128)S(1)} %bitcast.123, f32[8,256]{1,0:T(8,128)S(1)} %sub.340, f32[8,256]{1,0:T(8,128)S(1)} %bitcast.124, f32[8,256]{1,0:T(8,128)S(1)} %sub.341, f32[8,256]{1,0:T(8,128)S(1)} %bitcast.125, ...), kind=kOutput, calls=%fused_computation.4.clone.1 | convolution fusion | flops 77987840 | bytes 1392681 | tf_op jit(solution)/shard_map/while/body/eval_jaxpr/pra,rab->prb/dot_general | solution.py:59
  137.0 0.6 dynamic_slice.24
  138.3 0.6 gather_fusion
  139.7 4.6 %fusion.68 = f32[64,8,256]{2,0,1:T(8,128)S(1)} fusion(f32[8]{0:T(128)S(1)} %get-tuple-element.300, f32[8,256]{1,0:T(8,128)S(1)} %sub.339, f32[8,256]{1,0:T(8,128)S(1)} %bitcast.123, f32[8,256]{1,0:T(8,128)S(1)} %sub.340, f32[8,256]{1,0:T(8,128)S(1)} %bitcast.124, f32[8,256]{1,0:T(8,128)S(1)} %sub.341, f32[8,256]{1,0:T(8,128)S(1)} %bitcast.125, ...), kind=kOutput, calls=%fused_computation.4.clone.1 | convolution fusion | flops 77987840 | bytes 1392681 | tf_op jit(solution)/shard_map/while/body/eval_jaxpr/pra,rab->prb/dot_general | solution.py:59
  144.3 0.6 dynamic_slice.24
  145.6 0.6 gather_fusion
  146.9 4.6 %fusion.68 = f32[64,8,256]{2,0,1:T(8,128)S(1)} fusion(f32[8]{0:T(128)S(1)} %get-tuple-element.300, f32[8,256]{1,0:T(8,128)S(1)} %sub.339, f32[8,256]{1,0:T(8,128)S(1)} %bitcast.123, f32[8,256]{1,0:T(8,128)S(1)} %sub.340, f32[8,256]{1,0:T(8,128)S(1)} %bitcast.124, f32[8,256]{1,0:T(8,128)S(1)} %sub.341, f32[8,256]{1,0:T(8,128)S(1)} %bitcast.125, ...), kind=kOutput, calls=%fused_computation.4.clone.1 | convolution fusion | flops 77987840 | bytes 1392681 | tf_op jit(solution)/shard_map/while/body/eval_jaxpr/pra,rab->prb/dot_general | solution.py:59
  151.6 0.6 dynamic_slice.24
  152.9 0.6 gather_fusion
  154.2 4.6 %fusion.68 = f32[64,8,256]{2,0,1:T(8,128)S(1)} fusion(f32[8]{0:T(128)S(1)} %get-tuple-element.300, f32[8,256]{1,0:T(8,128)S(1)} %sub.339, f32[8,256]{1,0:T(8,128)S(1)} %bitcast.123, f32[8,256]{1,0:T(8,128)S(1)} %sub.340, f32[8,256]{1,0:T(8,128)S(1)} %bitcast.124, f32[8,256]{1,0:T(8,128)S(1)} %sub.341, f32[8,256]{1,0:T(8,128)S(1)} %bitcast.125, ...), kind=kOutput, calls=%fused_computation.4.clone.1 | convolution fusion | flops 77987840 | bytes 1392681 | tf_op jit(solution)/shard_map/while/body/eval_jaxpr/pra,rab->prb/dot_general | solution.py:59
  158.8 0.6 dynamic_slice.24
  160.2 0.6 gather_fusion
  161.5 4.6 %fusion.68 = f32[64,8,256]{2,0,1:T(8,128)S(1)} fusion(f32[8]{0:T(128)S(1)} %get-tuple-element.300, f32[8,256]{1,0:T(8,128)S(1)} %sub.339, f32[8,256]{1,0:T(8,128)S(1)} %bitcast.123, f32[8,256]{1,0:T(8,128)S(1)} %sub.340, f32[8,256]{1,0:T(8,128)S(1)} %bitcast.124, f32[8,256]{1,0:T(8,128)S(1)} %sub.341, f32[8,256]{1,0:T(8,128)S(1)} %bitcast.125, ...), kind=kOutput, calls=%fused_computation.4.clone.1 | convolution fusion | flops 77987840 | bytes 1392681 | tf_op jit(solution)/shard_map/while/body/eval_jaxpr/pra,rab->prb/dot_general | solution.py:59
  166.1 0.6 dynamic_slice.24
  167.4 0.6 gather_fusion
  168.8 4.6 %fusion.68 = f32[64,8,256]{2,0,1:T(8,128)S(1)} fusion(f32[8]{0:T(128)S(1)} %get-tuple-element.300, f32[8,256]{1,0:T(8,128)S(1)} %sub.339, f32[8,256]{1,0:T(8,128)S(1)} %bitcast.123, f32[8,256]{1,0:T(8,128)S(1)} %sub.340, f32[8,256]{1,0:T(8,128)S(1)} %bitcast.124, f32[8,256]{1,0:T(8,128)S(1)} %sub.341, f32[8,256]{1,0:T(8,128)S(1)} %bitcast.125, ...), kind=kOutput, calls=%fused_computation.4.clone.1 | convolution fusion | flops 77987840 | bytes 1392681 | tf_op jit(solution)/shard_map/while/body/eval_jaxpr/pra,rab->prb/dot_general | solution.py:59
  173.7 0.8 copy.36
  (288 shorter events, 21.7 us)
Async XLA Ops:
  0.0 173.4 %copy-start = (bf16[8,32,256]{2,1,0:T(8,128)(2,1)S(1)}, bf16[8,32,256]{2,1,0:T(8,128)(2,1)}, u32[]{:S(2)}) copy-start(bf16[8,32,256]{2,1,0:T(8,128)(2,1)} %param.14) | copy-start | bytes 393220
  0.0 37.9 %copy-start.4 = (s32[8,16]{1,0:T(8,128)S(1)}, s32[8,16]{1,0:T(8,128)}, u32[]{:S(2)}) copy-start(s32[8,16]{1,0:T(8,128)} %param.12) | copy-start | bytes 1540
  0.8 55.3 %collective-permute-start.1 = (f32[4,2048]{1,0:T(4,128)S(1)}, f32[4,2048]{1,0:T(4,128)S(1)}, u32[]{:S(2)}, u32[]{:S(2)}) collective-permute-start(f32[4,2048]{1,0:T(4,128)S(1)} %pad_maximum_fusion.2), channel_id=1, source_target_pairs={{1,0},{2,1},{3,2},{4,3},{5,4},{6,5},{7,6},{8,7},{9,8},{10,9},{11,1... | collective-permute-start | bytes 98312 | tf_op jit(solution)/shard_map/ppermute | solution.py:19
  2.1 54.0 %collective-permute-start = (f32[4,2048]{1,0:T(4,128)S(1)}, f32[4,2048]{1,0:T(4,128)S(1)}, u32[]{:S(2)}, u32[]{:S(2)}) collective-permute-start(f32[4,2048]{1,0:T(4,128)S(1)} %pad_maximum_fusion.2), channel_id=1, source_target_pairs={{0,1},{1,2},{2,3},{3,4},{4,5},{5,6},{6,7},{7,8},{8,9},{9,10},{10,1... | collective-permute-start | bytes 98312 | tf_op jit(solution)/shard_map/ppermute | solution.py:17
  5.2 51.0 %collective-permute-start.3 = (bf16[64,2048]{1,0:T(8,128)(2,1)}, bf16[64,2048]{1,0:T(8,128)(2,1)S(1)}, u32[]{:S(2)}, u32[]{:S(2)}) collective-permute-start(bf16[64,2048]{1,0:T(8,128)(2,1)} %param.11), channel_id=1, source_target_pairs={{1,0},{2,1},{3,2},{4,3},{5,4},{6,5},{7,6},{8,7},{9,8},{10,9},{11,1... | collective-permute-start | bytes 786440 | tf_op jit(solution)/shard_map/ppermute | solution.py:19
  6.5 49.8 %collective-permute-start.2 = (bf16[64,2048]{1,0:T(8,128)(2,1)}, bf16[64,2048]{1,0:T(8,128)(2,1)S(1)}, u32[]{:S(2)}, u32[]{:S(2)}) collective-permute-start(bf16[64,2048]{1,0:T(8,128)(2,1)} %param.11), channel_id=1, source_target_pairs={{0,1},{1,2},{2,3},{3,4},{4,5},{5,6},{6,7},{7,8},{8,9},{9,10},{10,1... | collective-permute-start | bytes 786440 | tf_op jit(solution)/shard_map/ppermute | solution.py:17
  14.5 41.5 %copy-start.3 = (f32[2048]{0:T(1024)S(1)}, f32[2048]{0:T(1024)}, u32[]{:S(2)}) copy-start(f32[2048]{0:T(1024)} %param.10) | copy-start | bytes 24580
  14.6 41.6 %copy-start.2 = (f32[3,2048]{1,0:T(4,128)S(1)}, f32[3,2048]{1,0:T(4,128)}, u32[]{:S(2)}) copy-start(f32[3,2048]{1,0:T(4,128)} %param.9) | copy-start | bytes 73732
  14.6 41.6 %copy-start.1 = (bf16[64,2048]{1,0:T(8,128)(2,1)S(1)}, bf16[64,2048]{1,0:T(8,128)(2,1)}, u32[]{:S(2)}) copy-start(bf16[64,2048]{1,0:T(8,128)(2,1)} %param.11) | copy-start | bytes 786436
  56.3 0.7 copy-start.5
where the time goes:
time: 175 us
  matrix products  75.7 us (43%)
  blocking collectives  40.8 us (23%)
  local copies, waits for them, and re-layouts  33.2 us (19%)
  other arithmetic  11.9 us (7%)
  starting transfers between devices  10.8 us (6%)
  loops' own time  1.93 us (1%)
    dot_general x16, matrix products, near_step(): jnp.einsum('pra,rab->prb', source_probe, tiles, preferred_element_type=jn...  73.9 us
    all_gather x1, blocking collectives, shards(): piece = lax.all_gather(folded, 'row', axis=0, tiled=True)  23.3 us
    all_gather x1, blocking collectives, shards(): all_centers = lax.all_gather(own_center, 'row', axis=1, tiled=True)  17.5 us
    dynamic_slice x16, local copies, waits for them, and re-layouts, shards(): near, _ = lax.scan(near_step, start_near, (near_ids.T, columns))  9.33 us
    gather x16, local copies, waits for them, and re-layouts, near_step(): source = jnp.take(rec_blocks, local_ids, axis=1)  9.23 us
    convert_element_type x16, other arithmetic, near_step(): keep = (column_index < near_count).astype(jnp.float32)  9.16 us
    gather x16, local copies, waits for them, and re-layouts, near_step(): source_probe = jnp.take(probe_blocks, local_ids, axis=1)  9.02 us
    ppermute x2, starting transfers between devices, with_halo(): lax.ppermute(tail, axis, [(i, (i + 1) % count) for i in range(ends)])  8.2 us
  transfers between devices with their start and end apart: 4, of which 0 were waited for; matrix products, arithmetic and copies ran while one was open for 2% of the time, Pallas kernels for 0%

commit v1 on v0

v1 whole, which is shorter than its diff:
```python
import functools
import math

import jax
import jax.numpy as jnp
from jax import lax
from jax.experimental import pallas as pl
from jax.experimental.pallas import tpu as pltpu
from jax.sharding import PartitionSpec as P

HALO = 8
ROWS = 16
LOG2E = 1.0 / math.log(2.0)
C_SCALE = math.log(2.0) ** (-2.0 / 3.0)
D_SCALE = 3.0 * LOG2E * LOG2E * C_SCALE
F32 = jnp.float32
BF16 = jnp.bfloat16


def split3(x):
    high = x.astype(BF16)
    rest = x - high.astype(F32)
    mid = rest.astype(BF16)
    low = (rest - mid.astype(F32)).astype(BF16)
    return high, mid, low


def left_stack(x):
    h, m, l = [part.astype(F32) for part in split3(x)]
    return jnp.concatenate([h, h, m, h, l, m, m, l], axis=0)


def right_stack(x):
    h, m, l = split3(x)
    return jnp.concatenate([h, m, h, l, h, m, l, m], axis=0)


def matern(first, second):
    sq_dist = (first[0] - second[0]) * (first[0] - second[0])
    sq_dist = sq_dist + (first[1] - second[1]) * (first[1] - second[1])
    sq_dist = sq_dist + (first[2] - second[2]) * (first[2] - second[2])
    mean_sq = 0.5 * (first[3] * first[3] + second[3] * second[3])
    ratio = first[3] * second[3] / mean_sq
    prefac = ratio * jnp.sqrt(ratio)
    scaled = jnp.sqrt(3.0 * (sq_dist / mean_sq))
    return prefac * (1.0 + scaled) * jnp.exp(-scaled)


def nt(a, b):
    return lax.dot_general(a, b, (((1,), (1,)), ((), ())), preferred_element_type=F32)


def tn(a, b):
    return lax.dot_general(a, b, (((0,), (0,)), ((), ())), preferred_element_type=F32)


def nn(a, b):
    return lax.dot_general(a, b, (((1,), (0,)), ((), ())), preferred_element_type=F32)


def kernel(
    n, ob, bs,
    xyz_ref, len_ref, probes_ref, ids_ref, bout_ref, bin_ref, out_ref,
    xyz_r, len_r, probes_r, ids_r,
    rec_i, rec_j, cen_i, cen_j, lhs, rhs_c, mask_a, mask_b, acc, part,
    fold_all, cen_all,
    halo_send, halo_recv, part_send, part_recv, gat_send, gat_recv, cen_send, cen_recv,
):
    me = lax.axis_index("row")
    left = lax.rem(me + n - 1, n)
    right = lax.rem(me + 1, n)
    half = bin_ref.shape[1] // 2
    np_ = probes_ref.shape[0]
    width = n * ob

    barrier = pltpu.get_barrier_semaphore()

    def greet(k, carry):
        pl.semaphore_signal(barrier, inc=1, device_id={"row": lax.rem(me + k, n)})
        return carry

    lax.fori_loop(1, n, greet, 0)
    pl.semaphore_wait(barrier, n - 1)

    halo = [
        pltpu.make_async_remote_copy(
            src_ref=src, dst_ref=dst, send_sem=halo_send.at[k], recv_sem=halo_recv.at[k], device_id={"row": left}
        )
        for k, (src, dst) in enumerate(
            ((xyz_ref, xyz_r), (len_ref, len_r), (ids_ref, ids_r), (probes_ref, probes_r))
        )
    ]
    for copy in halo:
        copy.start()

    row = lax.broadcasted_iota(jnp.int32, (ROWS, bs), 0)

    def fill_j(xyz, length, base):
        rec_j[0:3, base : base + ob * bs] = xyz[...]
        rec_j[3:6, base : base + ob * bs] = jnp.ones((3, ob * bs), F32)
        rec_j[6:9, base : base + ob * bs] = xyz[...]
        rec_j[9:10, base : base + ob * bs] = jnp.ones((1, ob * bs), F32)
        ln = length[...]
        rec_j[10:11, base : base + ob * bs] = ln * ln
        rec_j[11:12, base : base + ob * bs] = 1.0 / ln
        rec_j[12:16, base : base + ob * bs] = jnp.zeros((4, ob * bs), F32)
        for b in range(ob):
            at = base + b * bs
            blk = rec_j[:, at : at + bs]
            inv = rec_j[11:12, at : at + bs]
            feat = jnp.where((row == 9) | (row == 10), blk, 0.0) * (inv * (0.5 * C_SCALE))
            rhs_c[base // bs + b] = right_stack(feat)

    rec_i[0:3, :] = xyz_ref[...]
    rec_i[3:6, :] = xyz_ref[...]
    rec_i[6:9, :] = jnp.ones((3, ob * bs), F32)
    ln0 = len_ref[...]
    rec_i[9:10, :] = ln0 * ln0
    rec_i[10:11, :] = jnp.ones((1, ob * bs), F32)
    rec_i[11:12, :] = ln0
    rec_i[12:16, :] = jnp.zeros((4, ob * bs), F32)
    fill_j(xyz_ref, len_ref, 0)

    lane = lax.broadcasted_iota(jnp.int32, (ROWS, 128), 1)
    own_centers = jnp.zeros((ROWS, 128), F32)
    for b in range(ob):
        blk = rec_i[:, b * bs : (b + 1) * bs]
        mean = jnp.sum(blk, axis=1, keepdims=True) * (1.0 / bs)
        own_centers = jnp.where(lane == b, mean, own_centers)
        mean_w = jnp.broadcast_to(mean, (ROWS, bs))
        cen = jnp.where(row < 6, mean_w, 0.0)
        v = blk - cen
        feat = jnp.where((row >= 3) & (row < 6), v * v, jnp.where(row < 11, v, 0.0)) * (1.0 / rec_i[11:12, b * bs : (b + 1) * bs])
        lhs[b] = left_stack(feat).T.astype(BF16)
        mean_j = jnp.sum(rec_j[:, b * bs : (b + 1) * bs], axis=1, keepdims=True) * (1.0 / bs)
        cen_j[b] = jnp.where((row < 3) | ((row >= 6) & (row < 9)), jnp.broadcast_to(mean_j, (ROWS, bs)), 0.0)
        pb = probes_ref[:, b * bs : (b + 1) * bs]
        fold = jnp.concatenate([nt(bin_ref[b, 0:half, :], pb), nt(bin_ref[b, half:, :], pb)], axis=1)
        fold_all[me, b * half : (b + 1) * half, :] = fold.astype(BF16)
    square = jnp.concatenate([own_centers, jnp.zeros((128 - ROWS, 128), F32)], axis=0).T
    own_cols = square[0:ob, :]
    cen_all[me] = own_cols

    def gather_copies(k):
        peer = lax.rem(me + k, n)
        return (
            pltpu.make_async_remote_copy(
                src_ref=fold_all.at[me], dst_ref=fold_all.at[me],
                send_sem=gat_send.at[k], recv_sem=gat_recv.at[k], device_id={"row": peer},
            ),
            pltpu.make_async_remote_copy(
                src_ref=cen_all.at[me], dst_ref=cen_all.at[me],
                send_sem=cen_send.at[k], recv_sem=cen_recv.at[k], device_id={"row": peer},
            ),
        )

    def gather_start(k, carry):
        for copy in gather_copies(k):
            copy.start()
        return carry

    lax.fori_loop(1, n, gather_start, 0)

    acc[...] = jnp.zeros_like(acc)

    def member(ids, target):
        return jnp.max(jnp.where(ids == target, 1.0, 0.0), axis=1, keepdims=True)

    def store_rows(ref, base, value):
        wide = jnp.broadcast_to(value, (ob, bs))
        for b in range(ob):
            ref[base + b] = wide[b : b + 1, :]

    ids = ids_ref[...]
    gid = lax.broadcasted_iota(jnp.int32, ids.shape, 0) + me * ob
    for dj in range(HALO + 1):
        store_rows(mask_a, dj * ob, member(ids, gid + dj))
        if dj:
            store_rows(mask_b, dj * 2 * ob, member(ids, gid - dj))
        else:
            store_rows(mask_b, 0, jnp.zeros((ob, 1), F32))

    def tile(i, jw, p_ref, p_base):
        dj = jw - i
        at = pl.multiple_of(jw * bs, bs)
        blk = rec_j[:, pl.ds(at, bs)]
        inv = rec_j[11:12, pl.ds(at, bs)]
        v = blk - cen_j[i]
        feat = jnp.where(
            row < 3, (-2.0 * D_SCALE) * v,
            jnp.where(row < 6, D_SCALE, jnp.where(row < 9, D_SCALE * v * v, 0.0)),
        ) * inv
        both = nn(lhs[i], jnp.concatenate([right_stack(feat), rhs_c[jw]], axis=1))
        dist = both[:, :bs]
        w = lax.rsqrt(both[:, bs:])
        w2 = w * w
        u = jnp.maximum(dist * w2, 1e-30)
        s = u * lax.rsqrt(u)
        value = ((w2 * w) * (LOG2E + s)) * jnp.exp2(-s)
        value = value.astype(BF16)
        p_j = p_ref[:, pl.ds(pl.multiple_of(p_base * bs, bs), bs)]
        p_i = probes_ref[:, pl.ds(pl.multiple_of(i * bs, bs), bs)]
        return (
            mask_a[dj * ob + i] * nt(p_j, value),
            mask_b[dj * 2 * ob + jw] * nn(p_i, value),
        )

    def triangle(g, s):
        c = (s + g) // ob
        a = g + c * (ob - 1 - 2 * g)
        return a, a + s - c * (ob - g)

    def own_group(g, carry):
        def step(s, inner):
            i, j = triangle(g, s)
            first, second = tile(i, j, probes_ref, j)
            acc[i] += first
            acc[j] += second
            return inner

        return lax.fori_loop(0, ob + 1, step, carry)

    lax.fori_loop(0, ob // 4, own_group, 0)

    for copy in halo:
        copy.wait()
    fill_j(xyz_r, len_r, ob * bs)
    ids2 = ids_r[...]
    for dj in range(1, HALO + 1):
        store_rows(mask_b, dj * 2 * ob + ob, member(ids2, gid + ob - dj))

    def part_copy(col):
        return pltpu.make_async_remote_copy(
            src_ref=acc.at[ob + col], dst_ref=part.at[col],
            send_sem=part_send.at[col], recv_sem=part_recv.at[col], device_id={"row": right},
        )

    def cross_group(g, carry):
        def step(s, inner):
            col, i = triangle(g, s)
            first, second = tile(i, ob + col, probes_r, col)
            acc[i] += first
            acc[ob + col] += second
            return inner

        lax.fori_loop(0, ob + 1, step, 0)
        part_copy(g).start()
        part_copy(ob - 1 - g).start()
        return carry

    lax.fori_loop(0, ob // 2, cross_group, 0)
    lax.fori_loop(ob // 4, ob // 2, own_group, 0)

    def gather_wait(k, carry):
        for copy in gather_copies(k):
            copy.wait()
        return carry

    lax.fori_loop(1, n, gather_wait, 0)
    centers = cen_all[...].reshape(width, 128).T
    picks = (0, 1, 2, 11)
    coupling = matern([own_cols[:, c : c + 1] for c in picks], [centers[c : c + 1, :] for c in picks])
    global_ids = lax.broadcasted_iota(jnp.int32, (ob, width), 1)
    near = jnp.zeros((ob, width), F32)
    for t in range(ids.shape[1]):
        near = jnp.where(ids[:, t : t + 1] == global_ids, 1.0, near)
    coupling = jnp.where(near > 0.0, 0.0, coupling).astype(BF16)

    step_w = 128
    total = jnp.zeros((ob * half, 2 * np_), F32)
    pick_r = lax.broadcasted_iota(jnp.int32, (step_w, step_w * half), 0)
    pick_c = lax.broadcasted_iota(jnp.int32, (step_w, step_w * half), 1)
    spread = jnp.where(pick_c // half == pick_r, 1.0, 0.0).astype(BF16)
    eye_r = lax.broadcasted_iota(jnp.int32, (ob * half, step_w * half), 0)
    eye_c = lax.broadcasted_iota(jnp.int32, (ob * half, step_w * half), 1)
    same = lax.rem(eye_r, half) == lax.rem(eye_c, half)
    per = step_w // ob
    for q in range(width // step_w):
        wide = nn(coupling[:, q * step_w : (q + 1) * step_w], spread)
        wide = jnp.concatenate(
            [jnp.broadcast_to(wide[i : i + 1, :], (half, step_w * half)) for i in range(ob)], axis=0
        )
        kron = jnp.where(same, wide, 0.0).astype(BF16)
        folded = fold_all[q * per : (q + 1) * per].reshape(step_w * half, 2 * np_)
        total = total + nn(kron, folded)
    summed = total.astype(BF16)

    for b in range(ob):
        part_copy(b).wait()
    for b in range(ob):
        mine = summed[b * half : (b + 1) * half, :]
        far = tn(mine[:, :np_], bout_ref[b, 0:half, :]) + tn(mine[:, np_:], bout_ref[b, half:, :])
        out_ref[:, b * bs : (b + 1) * bs] = acc[b] + part[b] + far


def solution(mesh):
    n = mesh.shape["row"]

    def shards(coordinates, length_scale, probes, near_ids, near_count, basis_out, basis_in):
        ob, rank, bs = basis_out.shape
        np_ = probes.shape[0]
        own = ob * bs
        slots = near_ids.shape[1]
        vmem = pl.BlockSpec(memory_space=pltpu.VMEM)
        dma = pltpu.SemaphoreType.DMA
        return pl.pallas_call(
            functools.partial(kernel, n, ob, bs),
            out_shape=jax.ShapeDtypeStruct((np_, own), F32),
            in_specs=[vmem] * 6,
            out_specs=vmem,
            scratch_shapes=[
                pltpu.VMEM((3, own), F32),
                pltpu.VMEM((1, own), F32),
                pltpu.VMEM((np_, own), BF16),
                pltpu.VMEM((ob, slots), jnp.int32),
                pltpu.VMEM((ROWS, own), F32),
                pltpu.VMEM((ROWS, 2 * own), F32),
                pltpu.VMEM((ob, ROWS, bs), F32),
                pltpu.VMEM((ob, ROWS, bs), F32),
                pltpu.VMEM((ob, bs, 8 * ROWS), BF16),
                pltpu.VMEM((2 * ob, 8 * ROWS, bs), BF16),
                pltpu.VMEM(((HALO + 1) * ob, 1, bs), F32),
                pltpu.VMEM(((HALO + 1) * 2 * ob, 1, bs), F32),
                pltpu.VMEM((2 * ob, np_, bs), F32),
                pltpu.VMEM((ob, np_, bs), F32),
                pltpu.VMEM((n, ob * rank // 2, 2 * np_), BF16),
                pltpu.VMEM((n, ob, 128), F32),
                dma((4,)), dma((4,)), dma((ob,)), dma((ob,)),
                dma((n,)), dma((n,)), dma((n,)), dma((n,)),
            ],
            compiler_params=pltpu.CompilerParams(collective_id=0, has_side_effects=True, vmem_limit_bytes=48 * 1024 * 1024),
        )(coordinates, length_scale.reshape(1, own), probes, near_ids, basis_out, basis_in)

    placed = (
        P(None, ("grp", "row")),
        P(("grp", "row")),
        P(None, ("grp", "row")),
        P(("grp", "row"), None),
        P(("grp", "row")),
        P(("grp", "row"), None, None),
        P(("grp", "row"), None, None),
    )
    return jax.shard_map(
        shards, mesh=mesh, in_specs=placed, out_specs=P(None, ("grp", "row")), check_vma=False
    )
```

time: 175 us -> 49.6 us (0.28)
  the two profiles are of different devices: /device:TPU:0 before, /device:TPU:13 now
where the time goes in v1:
time: 49.6 us; the launch traced here: 49.3 us
  Pallas kernels  43.6 us (88%)
  local copies, waits for them, and re-layouts  5.69 us (11%)
    pallas_call x1, Pallas kernels, shards(): pl.pallas_call(functools.partial(kernel, n, ob, bs), out_shape=jax.ShapeD...  43.6 us
    unnamed x13, local copies, waits for them, and re-layouts  5.69 us

profile of v1, /device:TPU:13, one launch (start us, length us, event | category | flops | bytes accessed | tf_op | source)
XLA Modules:
  0.0 49.3 jit_solution(8245564008698179405)
XLA Ops:
  0.0 0.0 copy-start
  0.0 0.9 %copy-done = bf16[64,2048]{1,0:T(8,128)(2,1)S(1)} copy-done((bf16[64,2048]{1,0:T(8,128)(2,1)S(1)}, bf16[64,2048]{1,0:T(8,128)(2,1)}, u32[]{:S(2)}) %copy-start) | copy-done | bytes 262168
  1.0 0.0 copy-start.1
  1.0 0.9 %copy-done.1 = bf16[8,32,256]{2,1,0:T(8,128)(2,1)S(1)} copy-done((bf16[8,32,256]{2,1,0:T(8,128)(2,1)S(1)}, bf16[8,32,256]{2,1,0:T(8,128)(2,1)}, u32[]{:S(2)}) %copy-start.1) | copy-done | bytes 131096
  1.9 0.0 copy-start.2
  1.9 0.9 %copy-done.2 = bf16[8,32,256]{2,1,0:T(8,128)(2,1)S(1)} copy-done((bf16[8,32,256]{2,1,0:T(8,128)(2,1)S(1)}, bf16[8,32,256]{2,1,0:T(8,128)(2,1)}, u32[]{:S(2)}) %copy-start.2) | copy-done | bytes 131096
  2.8 0.0 copy-start.3
  2.8 0.8 %copy-done.3 = f32[3,2048]{1,0:T(4,128)S(1)} copy-done((f32[3,2048]{1,0:T(4,128)S(1)}, f32[3,2048]{1,0:T(4,128)}, u32[]{:S(2)}) %copy-start.3) | copy-done | bytes 24600
  3.5 0.0 copy-start.4
  3.5 0.7 %copy-done.4 = f32[2048]{0:T(1024)S(1)} copy-done((f32[2048]{0:T(1024)S(1)}, f32[2048]{0:T(1024)}, u32[]{:S(2)}) %copy-start.4) | copy-done | bytes 8216
  4.2 0.0 copy-start.5
  4.2 0.7 %copy-done.5 = s32[8,16]{1,0:T(8,128)S(1)} copy-done((s32[8,16]{1,0:T(8,128)S(1)}, s32[8,16]{1,0:T(8,128)}, u32[]{:S(2)}) %copy-start.5) | copy-done | bytes 536
  4.9 43.6 %shard_map.64 = f32[64,2048]{1,0:T(8,128)S(1)} custom-call(f32[3,2048]{1,0:T(4,128)S(1)} %copy-done.3, f32[1,2048]{1,0:T(1,128)S(1)} %bitcast.1, bf16[64,2048]{1,0:T(8,128)(2,1)S(1)} %copy-done, s32[8,16]{1,0:T(8,128)S(1)} %copy-done.5, bf16[8,32,256]{2,1,0:T(8,128)(2,1)S(1)} %copy-done.1, bf16[8,32,256]{2,1,0:T(8,128)(2,1)S(1)} %copy-done.2), custom_call_target="tpu_custom_call" | custom-call | tf_op jit(solution)/shard_map/pallas_call | solution.py:306
  48.5 0.8 %copy.8 = f32[64,2048]{1,0:T(8,128)} copy(f32[64,2048]{1,0:T(8,128)S(1)} %shard_map.64) | data formatting | bytes 1048576
Async XLA Ops:
  0.0 0.9 %copy-start = (bf16[64,2048]{1,0:T(8,128)(2,1)S(1)}, bf16[64,2048]{1,0:T(8,128)(2,1)}, u32[]{:S(2)}) copy-start(bf16[64,2048]{1,0:T(8,128)(2,1)} %probes_ref.1) | copy-start | bytes 786436
  1.0 0.9 %copy-start.1 = (bf16[8,32,256]{2,1,0:T(8,128)(2,1)S(1)}, bf16[8,32,256]{2,1,0:T(8,128)(2,1)}, u32[]{:S(2)}) copy-start(bf16[8,32,256]{2,1,0:T(8,128)(2,1)} %bout_ref.1) | copy-start | bytes 393220
  1.9 0.9 %copy-start.2 = (bf16[8,32,256]{2,1,0:T(8,128)(2,1)S(1)}, bf16[8,32,256]{2,1,0:T(8,128)(2,1)}, u32[]{:S(2)}) copy-start(bf16[8,32,256]{2,1,0:T(8,128)(2,1)} %bin_ref.1) | copy-start | bytes 393220
  2.8 0.8 %copy-start.3 = (f32[3,2048]{1,0:T(4,128)S(1)}, f32[3,2048]{1,0:T(4,128)}, u32[]{:S(2)}) copy-start(f32[3,2048]{1,0:T(4,128)} %xyz_ref.1) | copy-start | bytes 73732
  3.5 0.7 %copy-start.4 = (f32[2048]{0:T(1024)S(1)}, f32[2048]{0:T(1024)}, u32[]{:S(2)}) copy-start(f32[2048]{0:T(1024)} %param.8) | copy-start | bytes 24580
  4.2 0.7 %copy-start.5 = (s32[8,16]{1,0:T(8,128)S(1)}, s32[8,16]{1,0:T(8,128)}, u32[]{:S(2)}) copy-start(s32[8,16]{1,0:T(8,128)} %ids_ref.1) | copy-start | bytes 1540

commit v2 on v1

--- a/solution.py
+++ b/solution.py
@@ -10,6 +10,7 @@
 
 HALO = 8
 ROWS = 16
+CHUNKS = 1
 LOG2E = 1.0 / math.log(2.0)
 C_SCALE = math.log(2.0) ** (-2.0 / 3.0)
 D_SCALE = 3.0 * LOG2E * LOG2E * C_SCALE
@@ -60,16 +61,28 @@
 
 def kernel(
     n, ob, bs,
-    xyz_ref, len_ref, probes_ref, ids_ref, bout_ref, bin_ref, out_ref,
+    xyz_in, len_in, probes_in, ids_in, bout_in, bin_in, out_ref,
+    xyz_ref, len_ref, probes_ref, ids_ref, bout_ref, bin_ref,
     xyz_r, len_r, probes_r, ids_r,
     rec_i, rec_j, cen_i, cen_j, lhs, rhs_c, mask_a, mask_b, acc, part,
     fold_all, cen_all,
-    halo_send, halo_recv, part_send, part_recv, gat_send, gat_recv, cen_send, cen_recv,
+    value_buf, load_sem, halo_send, halo_recv, part_send, part_recv, gat_send, gat_recv, cen_send, cen_recv,
 ):
     me = lax.axis_index("row")
     left = lax.rem(me + n - 1, n)
     right = lax.rem(me + 1, n)
     half = bin_ref.shape[1] // 2
+    loads = [
+        pltpu.make_async_copy(src, dst, load_sem.at[k])
+        for k, (src, dst) in enumerate(
+            (
+                (xyz_in, xyz_ref), (len_in, len_ref), (ids_in, ids_ref),
+                (probes_in, probes_ref), (bin_in, bin_ref), (bout_in, bout_ref),
+            )
+        )
+    ]
+    for load in loads:
+        load.start()
     np_ = probes_ref.shape[0]
     width = n * ob
 
@@ -87,12 +100,14 @@
             src_ref=src, dst_ref=dst, send_sem=halo_send.at[k], recv_sem=halo_recv.at[k], device_id={"row": left}
         )
         for k, (src, dst) in enumerate(
-            ((xyz_ref, xyz_r), (len_ref, len_r), (ids_ref, ids_r), (probes_ref, probes_r))
+            ((xyz_in, xyz_r), (len_in, len_r), (ids_in, ids_r), (probes_in, probes_r))
         )
     ]
     for copy in halo:
         copy.start()
 
+    for load in loads[:5]:
+        load.wait()
     row = lax.broadcasted_iota(jnp.int32, (ROWS, bs), 0)
 
     def fill_j(xyz, length, base):
@@ -180,30 +195,52 @@
         else:
             store_rows(mask_b, 0, jnp.zeros((ob, 1), F32))
 
-    def tile(i, jw, p_ref, p_base):
-        dj = jw - i
+    rows = bs // CHUNKS
+
+    def right_side(i, jw):
         at = pl.multiple_of(jw * bs, bs)
-        blk = rec_j[:, pl.ds(at, bs)]
-        inv = rec_j[11:12, pl.ds(at, bs)]
-        v = blk - cen_j[i]
+        v = rec_j[:, pl.ds(at, bs)] - cen_j[i]
         feat = jnp.where(
             row < 3, (-2.0 * D_SCALE) * v,
             jnp.where(row < 6, D_SCALE, jnp.where(row < 9, D_SCALE * v * v, 0.0)),
-        ) * inv
-        both = nn(lhs[i], jnp.concatenate([right_stack(feat), rhs_c[jw]], axis=1))
-        dist = both[:, :bs]
+        ) * rec_j[11:12, pl.ds(at, bs)]
+        return jnp.concatenate([right_stack(feat), rhs_c[jw]], axis=1)
+
+    def entries(i, side, c):
+        return nn(lhs[i, c * rows : (c + 1) * rows, :], side)
+
+    def values(both):
         w = lax.rsqrt(both[:, bs:])
         w2 = w * w
-        u = jnp.maximum(dist * w2, 1e-30)
+        u = jnp.maximum(both[:, :bs] * w2, 1e-30)
         s = u * lax.rsqrt(u)
-        value = ((w2 * w) * (LOG2E + s)) * jnp.exp2(-s)
-        value = value.astype(BF16)
+        return (((w2 * w) * (LOG2E + s)) * jnp.exp2(-s)).astype(BF16)
+
+    def products(i, jw, p_ref, p_base, slot):
+        dj = jw - i
+        value = value_buf[slot]
         p_j = p_ref[:, pl.ds(pl.multiple_of(p_base * bs, bs), bs)]
         p_i = probes_ref[:, pl.ds(pl.multiple_of(i * bs, bs), bs)]
-        return (
-            mask_a[dj * ob + i] * nt(p_j, value),
-            mask_b[dj * 2 * ob + jw] * nn(p_i, value),
-        )
+        acc[i] += mask_a[dj * ob + i] * nt(p_j, value)
+        acc[jw] += mask_b[dj * 2 * ob + jw] * nn(p_i, value)
+
+    def sweep(pairs, p_ref):
+        side = right_side(pairs[0][0], pairs[0][1])
+        current = [entries(pairs[0][0], side, c) for c in range(CHUNKS)]
+        for t, (i, jw, p_base) in enumerate(pairs):
+            upcoming = None
+            if t + 1 < len(pairs):
+                upcoming = right_side(pairs[t + 1][0], pairs[t + 1][1])
+            following = []
+            for c in range(CHUNKS):
+                if upcoming is not None:
+                    following.append(entries(pairs[t + 1][0], upcoming, c))
+                value_buf[t % 2, c * rows : (c + 1) * rows, :] = values(current[c])
+                if c == 0 and t:
+                    products(*pairs[t - 1][:2], p_ref, pairs[t - 1][2], (t - 1) % 2)
+            current = following
+        last = len(pairs) - 1
+        products(*pairs[last][:2], p_ref, pairs[last][2], last % 2)
 
     def triangle(g, s):
         c = (s + g) // ob
@@ -211,14 +248,12 @@
         return a, a + s - c * (ob - g)
 
     def own_group(g, carry):
-        def step(s, inner):
+        pairs = []
+        for s in range(ob + 1):
             i, j = triangle(g, s)
-            first, second = tile(i, j, probes_ref, j)
-            acc[i] += first
-            acc[j] += second
-            return inner
-
-        return lax.fori_loop(0, ob + 1, step, carry)
+            pairs.append((i, j, j))
+        sweep(pairs, probes_ref)
+        return carry
 
     lax.fori_loop(0, ob // 4, own_group, 0)
 
@@ -236,14 +271,11 @@
         )
 
     def cross_group(g, carry):
-        def step(s, inner):
+        pairs = []
+        for s in range(ob + 1):
             col, i = triangle(g, s)
-            first, second = tile(i, ob + col, probes_r, col)
-            acc[i] += first
-            acc[ob + col] += second
-            return inner
-
-        lax.fori_loop(0, ob + 1, step, 0)
+            pairs.append((i, ob + col, col))
+        sweep(pairs, probes_r)
         part_copy(g).start()
         part_copy(ob - 1 - g).start()
         return carry
@@ -285,6 +317,7 @@
         total = total + nn(kron, folded)
     summed = total.astype(BF16)
 
+    loads[5].wait()
     for b in range(ob):
         part_copy(b).wait()
     for b in range(ob):
@@ -306,9 +339,15 @@
         return pl.pallas_call(
             functools.partial(kernel, n, ob, bs),
             out_shape=jax.ShapeDtypeStruct((np_, own), F32),
-            in_specs=[vmem] * 6,
+            in_specs=[pl.BlockSpec(memory_space=pl.ANY)] * 6,
             out_specs=vmem,
             scratch_shapes=[
+                pltpu.VMEM((3, own), F32),
+                pltpu.VMEM((1, own), F32),
+                pltpu.VMEM((np_, own), BF16),
+                pltpu.VMEM((ob, slots), jnp.int32),
+                pltpu.VMEM((ob, rank, bs), BF16),
+                pltpu.VMEM((ob, rank, bs), BF16),
                 pltpu.VMEM((3, own), F32),
                 pltpu.VMEM((1, own), F32),
                 pltpu.VMEM((np_, own), BF16),
@@ -325,10 +364,11 @@
                 pltpu.VMEM((ob, np_, bs), F32),
                 pltpu.VMEM((n, ob * rank // 2, 2 * np_), BF16),
                 pltpu.VMEM((n, ob, 128), F32),
-                dma((4,)), dma((4,)), dma((ob,)), dma((ob,)),
+                pltpu.VMEM((2, bs, bs), BF16),
+                dma((6,)), dma((4,)), dma((4,)), dma((ob,)), dma((ob,)),
                 dma((n,)), dma((n,)), dma((n,)), dma((n,)),
             ],
-            compiler_params=pltpu.CompilerParams(collective_id=0, has_side_effects=True, vmem_limit_bytes=48 * 1024 * 1024),
+            compiler_params=pltpu.CompilerParams(collective_id=0, has_side_effects=True, vmem_limit_bytes=60 * 1024 * 1024),
         )(coordinates, length_scale.reshape(1, own), probes, near_ids, basis_out, basis_in)
 
     placed = (

time: 49.6 us -> 33.6 us (0.68)
  Pallas kernels: 43.6 us -> 31.5 us
  local copies, waits for them, and re-layouts: 5.69 us -> 1.87 us
    pallas_call x1, Pallas kernels: 43.6 us -> 31.5 us  [shards(): pl.pallas_call(functools.partial(kernel, n, ob, bs), out_shape=jax.ShapeD...]
    unnamed x13 -> x1, local copies, waits for them, and re-layouts: 5.69 us -> 1.87 us
where the time goes in v2:
time: 33.6 us; the launch traced here: 33.4 us
  Pallas kernels  31.5 us (94%)
  local copies, waits for them, and re-layouts  1.87 us (6%)
    pallas_call x1, Pallas kernels, shards(): pl.pallas_call(functools.partial(kernel, n, ob, bs), out_shape=jax.ShapeD...  31.5 us
    unnamed x1, local copies, waits for them, and re-layouts  1.87 us

profile of v2, /device:TPU:13, one launch (start us, length us, event | category | flops | bytes accessed | tf_op | source)
XLA Modules:
  0.0 33.4 jit_solution(8918103069060240411)
XLA Ops:
  0.0 31.5 %shard_map.64 = f32[64,2048]{1,0:T(8,128)} custom-call(f32[3,2048]{1,0:T(4,128)} %xyz_in.1, f32[1,2048]{1,0:T(1,128)} %bitcast.1, bf16[64,2048]{1,0:T(8,128)(2,1)} %probes_in.1, s32[8,16]{1,0:T(8,128)} %ids_in.1, bf16[8,32,256]{2,1,0:T(8,128)(2,1)} %bout_in.1, bf16[8,32,256]{2,1,0:T(8,128)(2,1)} %bin_in.1), custom_call_target="tpu_custom_call" | custom-call | tf_op jit(solution)/shard_map/pallas_call | solution.py:339
  31.5 1.9 %copy.8 = f32[64,2048]{1,0:T(8,128)} copy(f32[64,2048]{1,0:T(8,128)} %shard_map.64) | data formatting | bytes 1048576

commit v3 on v2

--- a/solution.py
+++ b/solution.py
@@ -247,15 +247,15 @@
         a = g + c * (ob - 1 - 2 * g)
         return a, a + s - c * (ob - g)
 
-    def own_group(g, carry):
+    def own_groups(first, last):
         pairs = []
-        for s in range(ob + 1):
-            i, j = triangle(g, s)
-            pairs.append((i, j, j))
+        for g in range(first, last):
+            for s in range(ob + 1):
+                i, j = triangle(g, s)
+                pairs.append((i, j, j))
         sweep(pairs, probes_ref)
-        return carry
-
-    lax.fori_loop(0, ob // 4, own_group, 0)
+
+    own_groups(0, ob // 4)
 
     for copy in halo:
         copy.wait()
@@ -270,18 +270,20 @@
             send_sem=part_send.at[col], recv_sem=part_recv.at[col], device_id={"row": right},
         )
 
-    def cross_group(g, carry):
+    def cross_groups(h, carry):
         pairs = []
-        for s in range(ob + 1):
-            col, i = triangle(g, s)
-            pairs.append((i, ob + col, col))
+        for g in (2 * h, 2 * h + 1):
+            for s in range(ob + 1):
+                col, i = triangle(g, s)
+                pairs.append((i, ob + col, col))
         sweep(pairs, probes_r)
-        part_copy(g).start()
-        part_copy(ob - 1 - g).start()
+        for g in (2 * h, 2 * h + 1):
+            part_copy(g).start()
+            part_copy(ob - 1 - g).start()
         return carry
 
-    lax.fori_loop(0, ob // 2, cross_group, 0)
-    lax.fori_loop(ob // 4, ob // 2, own_group, 0)
+    lax.fori_loop(0, ob // 4, cross_groups, 0)
+    own_groups(ob // 4, ob // 2)
 
     def gather_wait(k, carry):
         for copy in gather_copies(k):

time: 33.6 us -> 33.9 us (level)
  the two profiles are of different devices: /device:TPU:13 before, /device:TPU:16 now
where the time goes in v3:
time: 33.9 us; the launch traced here: 33.8 us
  Pallas kernels  31.9 us (94%)
  local copies, waits for them, and re-layouts  1.87 us (6%)
    pallas_call x1, Pallas kernels, shards(): pl.pallas_call(functools.partial(kernel, n, ob, bs), out_shape=jax.ShapeD...  31.9 us
    unnamed x1, local copies, waits for them, and re-layouts  1.87 us

profile of v3, /device:TPU:16, one launch (start us, length us, event | category | flops | bytes accessed | tf_op | source)
XLA Modules:
  0.0 33.8 jit_solution(17547491054303070135)
XLA Ops:
  0.0 31.9 %shard_map.64 = f32[64,2048]{1,0:T(8,128)} custom-call(f32[3,2048]{1,0:T(4,128)} %xyz_in.1, f32[1,2048]{1,0:T(1,128)} %bitcast.1, bf16[64,2048]{1,0:T(8,128)(2,1)} %probes_in.1, s32[8,16]{1,0:T(8,128)} %ids_in.1, bf16[8,32,256]{2,1,0:T(8,128)(2,1)} %bout_in.1, bf16[8,32,256]{2,1,0:T(8,128)(2,1)} %bin_in.1), custom_call_target="tpu_custom_call" | custom-call | tf_op jit(solution)/shard_map/pallas_call | solution.py:341
  31.9 1.9 %copy.8 = f32[64,2048]{1,0:T(8,128)} copy(f32[64,2048]{1,0:T(8,128)} %shard_map.64) | data formatting | bytes 1048576
